TPU v7x, 32 devices: a whole 2x2x4 slice. The times are simulated.
32 devices in a mesh: mom: 8 (over z, x), row: 2 (over core), col: 2 (over y).
Axes of the slice: x: 2, y: 2, z: 4, core: 2. Of those that a mesh axis runs over, the one named last changes fastest.
Arguments:
- left_part: bfloat16 [8, 1536, 1536], P('mom', 'row', 'col'), may hold values from -0.15625 to 0.15625
- vertex: bfloat16 [8, 1536, 1536], P('mom', 'row', 'col'), may hold values from -6 to 6
- bubble: float32 [8, 1536], P('mom'), may hold values from 0.25 to 2
- cross_map: int32 [1536, 8], P(('col', 'mom')), may hold values from 0 to 7, each once within a row
Outputs:
- crossed: bfloat16 [1536, 8, 1536], P(('col', 'mom'), None, 'row')
Inputs may be any that keep to these rules, and one draw needn't show every extreme that they name: Each row cross_map[b, :] is a permutation of the 8 transfer momenta.
All inputs are finite; a program needn't handle non-finite values.
Results may differ from a plain program's by a relative error of at most 0.0055.
Values may be sent and summed in bfloat16 or wider, within the bound.
No kernel may reach another device: no remote copies, remote signals or barrier semaphores. Data moves between devices by JAX's collectives and lax.ppermute only.
A program may use at most 64 MiB of HBM per device.

v0:
```python
import jax
import jax.numpy as jnp
from jax import lax
from jax.sharding import PartitionSpec as P


def on_device(left_part, vertex, bubble, cross_map):
    left_full = lax.all_gather(left_part, "col", axis=2, tiled=True)
    weighted = (left_full.astype(jnp.float32) * bubble[:, None, :]).astype(jnp.bfloat16)
    local_q = vertex.shape[0]
    col_count = vertex.shape[2]
    row_count = weighted.shape[1]
    momenta = lax.axis_size("mom")
    per_device = col_count // momenta
    sliced = weighted
    first_term = jnp.einsum(
        "qkb,qak->qba",
        lax.all_gather(vertex, "row", axis=1, tiled=True),
        sliced,
        preferred_element_type=jnp.float32,
    )
    first_round = first_term.astype(jnp.bfloat16)
    flipped = jnp.swapaxes(vertex, 1, 2).astype(jnp.float32)
    sliced = weighted
    second_term = jnp.einsum(
        "qbk,qak->qba",
        lax.all_gather(first_round, "row", axis=2, tiled=True),
        sliced,
        preferred_element_type=jnp.float32,
    )
    summed = (flipped + first_term + second_term).astype(jnp.bfloat16)
    summed = summed.reshape(local_q, momenta, per_device, row_count)
    received = lax.all_to_all(summed, "mom", split_axis=1, concat_axis=0, tiled=True)
    regrouped = received.reshape(-1, per_device, received.shape[-1])
    which = jnp.arange(per_device, dtype=jnp.int32)[:, None]
    return regrouped[cross_map, which]


def solution(mesh):
    in_specs = (
        P("mom", "row", "col"),
        P("mom", "row", "col"),
        P("mom", None),
        P(("col", "mom"), None),
    )
    out_specs = P(("col", "mom"), None, "row")
    return jax.shard_map(
        on_device, mesh=mesh, in_specs=in_specs, out_specs=out_specs, check_vma=False
    )
```

profile of v0, /device:TPU:0, one launch (start us, length us, event | category | flops | bytes accessed | tf_op | source)
XLA Modules:
  0.0 135.0 jit_solution(14771618672102993497)
XLA Ops:
  6.5 0.0 copy-start.1
  6.5 0.0 all-gather.5.cloned.1.call-start
  6.5 0.7 all-gather.5.cloned.1.call-update
  7.3 0.0 all-gather.7.cloned.1.call-start
  7.3 0.7 all-gather.7.cloned.1.call-update
  8.0 0.0 all-gather.9.cloned.1.call-start
  8.1 0.0 copy-done.1
  8.1 0.0 copy-start
  8.1 39.6 %all-gather.5.cloned.1.call-done = bf16[1,768,1536]{2,1,0:T(8,128)(2,1)} async-done(((bf16[1,768,768]{2,1,0:T(8,128)(2,1)}), bf16[1,768,1536]{2,1,0:T(8,128)(2,1)}) %all-gather.5.cloned.1.call-update) | async-done | bytes 2359312 | tf_op jit(solution)/shard_map/all_gather | solution.py:8
  47.7 12.5 %all-gather.7.cloned.1.call-done = bf16[1,1536,768]{2,1,0:T(8,128)(2,1)} async-done(((bf16[1,768,768]{2,1,0:T(8,128)(2,1)}), bf16[1,1536,768]{2,1,0:T(8,128)(2,1)}) %all-gather.7.cloned.1.call-update) | async-done | bytes 2359312 | tf_op jit(solution)/shard_map/all_gather | solution.py:18
  60.2 6.2 %bitcast_convert_fusion = (bf16[768,768]{1,0:T(8,128)(2,1)}, f32[768,768]{0,1:T(8,128)}) fusion(bf16[1,1536,768]{2,1,0:T(8,128)(2,1)} %all-gather.7.cloned.1.call-done, bf16[1,768,1536]{2,1,0:T(8,128)(2,1)} %all-gather.5.cloned.1.call-done, f32[1536]{0:T(1024)S(1)} %reduce), kind=kOutput, calls=%fused_computation.6 | convolution fusion | flops 1816068096 | bytes 8263680 | tf_op jit(solution)/shard_map/qkb,qak->qba/dot_general | solution.py:16
  66.4 0.0 all-gather.9.cloned.1.call-update
  66.5 0.0 copy-done
  66.5 0.6 copy.8
  67.1 11.6 %all-gather.9.cloned.1.call-done = bf16[768,1536]{1,0:T(8,128)(2,1)} async-done(((bf16[768,768]{1,0:T(8,128)(2,1)}), bf16[768,1536]{1,0:T(8,128)(2,1)}) %all-gather.9.cloned.1.call-update) | async-done | bytes 2359312 | tf_op jit(solution)/shard_map/all_gather | solution.py:27
  78.7 6.1 %fusion.2 = bf16[1,768,768]{2,1,0:T(8,128)(2,1)} fusion(f32[768,768]{0,1:T(8,128)} %get-tuple-element.6, bf16[1,768,768]{1,2,0:T(8,128)(2,1)S(1)} %copy.8, bf16[768,1536]{1,0:T(8,128)(2,1)} %all-gather.9.cloned.1.call-done, bf16[1,768,1536]{2,1,0:T(8,128)(2,1)} %all-gather.5.cloned.1.call-done, f32[1536]{0:T(1024)S(1)} %reduce), kind=kOutput, calls=%fused_computation.5 | convolution fusion | flops 1817837568 | bytes 9443328 | tf_op jit(solution)/shard_map/qbk,qak->qba/dot_general | solution.py:25
  84.9 0.0 copy-start.2
  84.9 5.9 %all-to-all-start = ((bf16[1,8,96,768]{3,2,0,1:T(8,128)(2,1)}), bf16[1,8,96,768]{3,2,0,1:T(8,128)(2,1)S(1)}, u32[]{:S(2)}, u32[]{:S(2)}) async-start(bf16[1,8,96,768]{3,2,0,1:T(8,128)(2,1)} %bitcast.7), calls=%async_computation | async-start | bytes 2359296 | tf_op jit(solution)/shard_map/all_to_all | solution.py:33
  90.8 0.0 copy-done.2
  90.8 0.1 copy.10
  90.9 0.1 reshape.33
  91.0 28.8 %all-to-all-done = bf16[1,8,96,768]{3,2,0,1:T(8,128)(2,1)S(1)} async-done(((bf16[1,8,96,768]{3,2,0,1:T(8,128)(2,1)}), bf16[1,8,96,768]{3,2,0,1:T(8,128)(2,1)S(1)}, u32[]{:S(2)}, u32[]{:S(2)}) %all-to-all-start) | async-done | bytes 1179680 | tf_op jit(solution)/shard_map/all_to_all | solution.py:33
  119.8 8.7 %gather_fusion = bf16[768,768]{1,0:T(8,128)(2,1)} fusion(bf16[8,96,768]{2,1,0:T(8,128)(2,1)S(1)} %bitcast.38, s32[768]{0:T(1024)S(1)} %reshape.33), kind=kCustom, calls=%fused_computation | custom fusion | bytes 2365440 | tf_op jit(solution)/shard_map/gather | solution.py:36
  (2 shorter events, 0.0 us)
Async XLA Ops:
  6.5 1.5 %copy-start.1 = (f32[1,1536]{1,0:T(1,128)S(1)}, f32[1,1536]{1,0:T(1,128)}, u32[]{:S(2)}) copy-start(f32[1,1536]{1,0:T(1,128)} %param.6) | copy-start | bytes 18436
  6.5 41.1 %all-gather.5.cloned.1.call-start = ((), (), s32[]{:S(2)}) async-start(), calls=%async_computation.1 | async-start | bytes 3538944 | tf_op jit(solution)/shard_map/all_gather | solution.py:8
  7.3 53.0 %all-gather.7.cloned.1.call-start = ((), (), s32[]{:S(2)}) async-start(), calls=%async_computation.2 | async-start | bytes 3538944 | tf_op jit(solution)/shard_map/all_gather | solution.py:18
  8.0 70.7 %all-gather.9.cloned.1.call-start = ((), (), s32[]{:S(2)}) async-start(), calls=%async_computation.3 | async-start | bytes 3538944 | tf_op jit(solution)/shard_map/all_gather | solution.py:27
  8.1 58.4 %copy-start = (bf16[1,768,768]{2,1,0:T(8,128)(2,1)S(1)}, bf16[1,768,768]{2,1,0:T(8,128)(2,1)}, u32[]{:S(2)}) copy-start(bf16[1,768,768]{2,1,0:T(8,128)(2,1)} %param.5) | copy-start | bytes 3538948
  84.9 5.9 %copy-start.2 = (s32[96,8]{0,1:T(8,128)S(1)}, s32[96,8]{0,1:T(8,128)}, u32[]{:S(2)}) copy-start(s32[96,8]{0,1:T(8,128)} %param.7) | copy-start | bytes 9220
  84.9 34.9 %all-to-all-start = ((bf16[1,8,96,768]{3,2,0,1:T(8,128)(2,1)}), bf16[1,8,96,768]{3,2,0,1:T(8,128)(2,1)S(1)}, u32[]{:S(2)}, u32[]{:S(2)}) async-start(bf16[1,8,96,768]{3,2,0,1:T(8,128)(2,1)} %bitcast.7), calls=%async_computation | async-start | bytes 2359296 | tf_op jit(solution)/shard_map/all_to_all | solution.py:33
Sparse Core Ops, SparseCore 0:
  8.9 38.7 all-gather.4
  49.2 10.9 all-gather.6
  66.6 12.1 all-gather.8
where the time goes:
time: 135 us
  waiting for transfers between devices  94 us (70%)
  between operations  13.2 us (10%)
  matrix products  12.3 us (9%)
  local copies, waits for them, and re-layouts  9.52 us (7%)
  starting transfers between devices  5.99 us (4%)
    all_gather x1, waiting for transfers between devices, on_device(): left_full = lax.all_gather(left_part, 'col', axis=2, tiled=True)  39.6 us
    all_to_all x1, waiting for transfers between devices, on_device(): lax.all_to_all(summed, 'mom', split_axis=1, concat_axis=0, tiled=True)  28.8 us
    all_gather x1, waiting for transfers between devices, on_device(): lax.all_gather(vertex, 'row', axis=1, tiled=True)  12.5 us
    all_gather x1, waiting for transfers between devices, on_device(): lax.all_gather(first_round, 'row', axis=2, tiled=True)  11.6 us
    gather x1, local copies, waits for them, and re-layouts, on_device(): return regrouped[cross_map, which]  8.68 us
    dot_general x1, matrix products, on_device(): jnp.einsum('qkb,qak->qba', lax.all_gather(vertex, 'row', axis=1, tiled=Tr...  6.21 us
    dot_general x1, matrix products, on_device(): jnp.einsum('qbk,qak->qba', lax.all_gather(first_round, 'row', axis=2, til...  6.14 us
    all_to_all x1, starting transfers between devices, on_device(): lax.all_to_all(summed, 'mom', split_axis=1, concat_axis=0, tiled=True)  5.91 us
  transfers between devices with their start and end apart: 4, of which 4 were waited for; matrix products, arithmetic and copies ran while one was open for 1% of the time, Pallas kernels for 0%

commit v1 on v0

--- a/solution.py
+++ b/solution.py
@@ -30,7 +30,10 @@
     )
     summed = (flipped + first_term + second_term).astype(jnp.bfloat16)
     summed = summed.reshape(local_q, momenta, per_device, row_count)
-    received = lax.all_to_all(summed, "mom", split_axis=1, concat_axis=0, tiled=True)
+    count = lax.axis_size("mom")
+    blocks = jnp.stack(jnp.split(summed, count, axis=1), axis=0)
+    blocks = lax.all_to_all(blocks, "mom", split_axis=0, concat_axis=0)
+    received = jnp.concatenate(blocks, axis=0)
     regrouped = received.reshape(-1, per_device, received.shape[-1])
     which = jnp.arange(per_device, dtype=jnp.int32)[:, None]
     return regrouped[cross_map, which]

time: 135 us -> 140 us (1.037)
  local copies, waits for them, and re-layouts: 9.52 us -> 16.1 us
    unnamed x7 -> x14, local copies, waits for them, and re-layouts: 0.66 us -> 6.58 us
where the time goes in v1:
time: 140 us; the launch traced here: 139 us
  waiting for transfers between devices  92.8 us (66%)
  local copies, waits for them, and re-layouts  16.1 us (12%)
  between operations  13.2 us (9%)
  matrix products  11.3 us (8%)
  starting transfers between devices  5.99 us (4%)
    all_gather x1, waiting for transfers between devices, on_device(): left_full = lax.all_gather(left_part, 'col', axis=2, tiled=True)  39.6 us
    all_to_all x1, waiting for transfers between devices, on_device(): blocks = lax.all_to_all(blocks, 'mom', split_axis=0, concat_axis=0)  28.8 us
    all_gather x1, waiting for transfers between devices, on_device(): lax.all_gather(vertex, 'row', axis=1, tiled=True)  12.5 us
    all_gather x1, waiting for transfers between devices, on_device(): lax.all_gather(first_round, 'row', axis=2, tiled=True)  10.4 us
    gather x1, local copies, waits for them, and re-layouts, on_device(): return regrouped[cross_map, which]  8.68 us
    unnamed x14, local copies, waits for them, and re-layouts  6.58 us
    dot_general x1, matrix products, on_device(): jnp.einsum('qkb,qak->qba', lax.all_gather(vertex, 'row', axis=1, tiled=Tr...  6.21 us
    all_to_all x1, starting transfers between devices, on_device(): blocks = lax.all_to_all(blocks, 'mom', split_axis=0, concat_axis=0)  5.91 us
  transfers between devices with their start and end apart: 4, of which 4 were waited for; matrix products, arithmetic and copies ran while one was open for 1% of the time, Pallas kernels for 0%

profile of v1, /device:TPU:0, one launch (start us, length us, event | category | flops | bytes accessed | tf_op | source)
XLA Modules:
  0.0 139.4 jit_solution(2156824598119331627)
XLA Ops:
  6.5 0.0 copy-start.1
  6.5 0.0 all-gather.5.cloned.1.call-start
  6.5 0.7 all-gather.5.cloned.1.call-update
  7.3 0.0 all-gather.7.cloned.1.call-start
  7.3 0.7 all-gather.7.cloned.1.call-update
  8.0 0.0 all-gather.9.cloned.1.call-start
  8.1 0.0 copy-done.1
  8.1 39.6 %all-gather.5.cloned.1.call-done = bf16[1,768,1536]{2,1,0:T(8,128)(2,1)} async-done(((bf16[1,768,768]{2,1,0:T(8,128)(2,1)}), bf16[1,768,1536]{2,1,0:T(8,128)(2,1)}) %all-gather.5.cloned.1.call-update) | async-done | bytes 2359312 | tf_op jit(solution)/shard_map/all_gather | solution.py:8
  47.7 12.5 %all-gather.7.cloned.1.call-done = bf16[1,1536,768]{2,1,0:T(8,128)(2,1)} async-done(((bf16[1,768,768]{2,1,0:T(8,128)(2,1)}), bf16[1,1536,768]{2,1,0:T(8,128)(2,1)}) %all-gather.7.cloned.1.call-update) | async-done | bytes 2359312 | tf_op jit(solution)/shard_map/all_gather | solution.py:18
  60.2 6.2 %bitcast_convert_fusion = (bf16[768,768]{1,0:T(8,128)(2,1)}, f32[768,768]{0,1:T(8,128)}) fusion(bf16[1,1536,768]{2,1,0:T(8,128)(2,1)} %all-gather.7.cloned.1.call-done, bf16[1,768,1536]{2,1,0:T(8,128)(2,1)} %all-gather.5.cloned.1.call-done, f32[1536]{0:T(1024)S(1)} %reduce), kind=kOutput, calls=%fused_computation.6 | convolution fusion | flops 1816068096 | bytes 8263680 | tf_op jit(solution)/shard_map/qkb,qak->qba/dot_general | solution.py:16
  66.4 0.0 copy-start
  66.4 0.0 all-gather.9.cloned.1.call-update
  66.5 1.2 copy-done
  67.7 0.6 copy.22
  68.3 10.4 %all-gather.9.cloned.1.call-done = bf16[768,1536]{1,0:T(8,128)(2,1)} async-done(((bf16[768,768]{1,0:T(8,128)(2,1)}), bf16[768,1536]{1,0:T(8,128)(2,1)}) %all-gather.9.cloned.1.call-update) | async-done | bytes 2359312 | tf_op jit(solution)/shard_map/all_gather | solution.py:27
  78.7 5.1 %fusion.2 = bf16[1,768,768]{2,1,0:T(8,128)(2,1)S(1)} fusion(f32[768,768]{0,1:T(8,128)} %get-tuple-element.6, bf16[1,768,768]{1,2,0:T(8,128)(2,1)S(1)} %copy.22, bf16[768,1536]{1,0:T(8,128)(2,1)} %all-gather.9.cloned.1.call-done, bf16[1,768,1536]{2,1,0:T(8,128)(2,1)} %all-gather.5.cloned.1.call-done, f32[1536]{0:T(1024)S(1)} %reduce), kind=kOutput, calls=%fused_computation.5 | convolution fusion | flops 1817837568 | bytes 9443328 | tf_op jit(solution)/shard_map/qbk,qak->qba/dot_general | solution.py:25
  83.9 0.7 fusion.17
  84.5 0.7 fusion.16
  85.2 0.7 fusion.15
  85.9 0.7 fusion.14
  86.6 0.7 fusion.13
  87.2 0.7 fusion.12
  87.9 0.7 fusion.11
  88.6 0.7 fusion.10
  89.2 0.0 copy-start.2
  89.2 5.9 %all-to-all-start = ((bf16[8,1,1,96,768]{4,3,2,1,0:T(8,128)(2,1)}), bf16[8,1,1,96,768]{4,3,2,1,0:T(8,128)(2,1)S(1)}, u32[]{:S(2)}, u32[]{:S(2)}) async-start(bf16[8,1,1,96,768]{4,3,2,1,0:T(8,128)(2,1)} %fusion.10), calls=%async_computation | async-start | bytes 2359296 | tf_op jit(solution)/shard_map/all_to_all | solution.py:35
  95.2 0.0 copy-done.2
  95.2 0.1 copy.23
  95.3 0.1 reshape.25
  95.4 28.8 %all-to-all-done = bf16[8,1,1,96,768]{4,3,2,1,0:T(8,128)(2,1)S(1)} async-done(((bf16[8,1,1,96,768]{4,3,2,1,0:T(8,128)(2,1)}), bf16[8,1,1,96,768]{4,3,2,1,0:T(8,128)(2,1)S(1)}, u32[]{:S(2)}, u32[]{:S(2)}) %all-to-all-start) | async-done | bytes 1179680 | tf_op jit(solution)/shard_map/all_to_all | solution.py:35
  124.2 8.7 %gather_fusion = bf16[768,768]{1,0:T(8,128)(2,1)} fusion(bf16[8,96,768]{2,1,0:T(8,128)(2,1)S(1)} %bitcast.68, s32[768]{0:T(1024)S(1)} %reshape.25), kind=kCustom, calls=%fused_computation | custom fusion | bytes 2365440 | tf_op jit(solution)/shard_map/gather | solution.py:39
  (2 shorter events, 0.0 us)
Async XLA Ops:
  6.5 1.5 %copy-start.1 = (f32[1,1536]{1,0:T(1,128)S(1)}, f32[1,1536]{1,0:T(1,128)}, u32[]{:S(2)}) copy-start(f32[1,1536]{1,0:T(1,128)} %param.6) | copy-start | bytes 18436
  6.5 41.1 %all-gather.5.cloned.1.call-start = ((), (), s32[]{:S(2)}) async-start(), calls=%async_computation.1 | async-start | bytes 3538944 | tf_op jit(solution)/shard_map/all_gather | solution.py:8
  7.3 53.0 %all-gather.7.cloned.1.call-start = ((), (), s32[]{:S(2)}) async-start(), calls=%async_computation.2 | async-start | bytes 3538944 | tf_op jit(solution)/shard_map/all_gather | solution.py:18
  8.0 70.7 %all-gather.9.cloned.1.call-start = ((), (), s32[]{:S(2)}) async-start(), calls=%async_computation.3 | async-start | bytes 3538944 | tf_op jit(solution)/shard_map/all_gather | solution.py:27
  66.4 1.3 copy-start
  89.2 5.9 %copy-start.2 = (s32[96,8]{0,1:T(8,128)S(1)}, s32[96,8]{0,1:T(8,128)}, u32[]{:S(2)}) copy-start(s32[96,8]{0,1:T(8,128)} %param.7) | copy-start | bytes 9220
  89.2 34.9 %all-to-all-start = ((bf16[8,1,1,96,768]{4,3,2,1,0:T(8,128)(2,1)}), bf16[8,1,1,96,768]{4,3,2,1,0:T(8,128)(2,1)S(1)}, u32[]{:S(2)}, u32[]{:S(2)}) async-start(bf16[8,1,1,96,768]{4,3,2,1,0:T(8,128)(2,1)} %fusion.10), calls=%async_computation | async-start | bytes 2359296 | tf_op jit(solution)/shard_map/all_to_all | solution.py:35
Sparse Core Ops, SparseCore 0:
  8.9 38.7 all-gather.4
  49.2 10.9 all-gather.6
  66.6 12.1 all-gather.8
